TPU v7x, 512 devices: a whole 4x8x8 slice. The times are simulated.
512 devices in a mesh: outer: 16 (over y, core), inner: 32 (over x, z).
Axes of the slice: x: 4, y: 8, z: 8, core: 2. Of those that a mesh axis runs over, the one named last changes fastest.
Arguments:
- queries: bfloat16 [32768, 4096], P('inner', 'outer'), may hold values from -150 to 150
- keys: bfloat16 [32768, 4096], P('inner', 'outer'), may hold values from -7 to 7
- values: bfloat16 [32768, 4096], P('inner', 'outer'), may hold values from -18 to 18
- counts: int32 [256], P('inner'), may hold values from 1 to 128, 24576 in all
- window_mask: int32 [256, 3], P('inner'), may hold values 0 or 1
- norm_gain: float32 [4096], P('outer'), may hold values from 0.5 to 1.5
Outputs:
- attended: bfloat16 [32768, 4096], P('inner', 'outer')
Inputs may be any that keep to these rules, and one draw needn't show every extreme that they name: `counts`: the largest count is exactly 128.
All inputs are finite; a program needn't handle non-finite values. No bound on the sum of `counts` or of `window_mask` on one device may be relied on, other than what follows from the above.
Results may differ from a plain program's by a relative error of at most 0.0048.
Values may be sent and summed in bfloat16 or wider, within the bound.
A program may use at most 64 MiB of HBM per device.

v0:
```python
import jax
import jax.numpy as jnp
from jax import lax
from jax.sharding import PartitionSpec as P

HD = 128
BLK = 128
PREV = 3
WIDTH = 4096


def carried_in(part, axis, combine, identity):
    place = lax.axis_index(axis)
    gathered = lax.all_gather(part, axis)
    state = jnp.zeros_like(part) + jnp.asarray(identity, part.dtype)

    def one(step, state):
        return combine(state, lax.dynamic_index_in_dim(gathered, step, 0, False))

    return lax.fori_loop(0, place, one, state)


def from_behind(value, axis, steps):
    count = lax.axis_size(axis)
    first, last = (max(0, -steps), min(count, count - steps))
    return lax.ppermute(value, axis, [(source, source + steps) for source in range(first, last)])


def add_states(earlier, later):
    return earlier + later


def shards(queries, keys, values, counts, window_mask, norm_gain):
    tok_rows = queries.shape[0]
    groups_here = tok_rows // BLK
    local_heads = queries.shape[1] // HD
    position = lax.broadcasted_iota(jnp.int32, (BLK,), 0)
    key_valid = position[None, :] < counts[:, None]
    masked_keys = jnp.where(key_valid.reshape(tok_rows)[:, None], keys, jnp.zeros((), jnp.bfloat16))
    query_blocks = queries.reshape(groups_here, BLK, local_heads, HD)
    key_blocks = masked_keys.reshape(groups_here, BLK, local_heads, HD)
    value_blocks = values.reshape(groups_here, BLK, local_heads, HD)
    group_states = jnp.einsum(
        "cshd,cshe->chde", key_blocks, value_blocks, preferred_element_type=jnp.float32
    )
    running = jnp.cumsum(group_states, axis=0)
    within = jnp.concatenate([jnp.zeros_like(group_states[:1]), running[:-1]], axis=0)
    span_total = running[-1]
    before = carried_in(span_total, "inner", add_states, jnp.zeros_like(span_total))
    prior_rounded = (before[None] + within).astype(jnp.bfloat16)
    rim_rows = PREV * BLK
    rim_keys, rim_values, rim_counts = from_behind(
        (
            masked_keys[tok_rows - rim_rows :],
            values[tok_rows - rim_rows :],
            counts[groups_here - PREV :],
        ),
        "inner",
        1,
    )
    extended_keys = jnp.concatenate([rim_keys, masked_keys], axis=0).reshape(
        groups_here + PREV, BLK, local_heads, HD
    )
    extended_values = jnp.concatenate([rim_values, values], axis=0).reshape(
        groups_here + PREV, BLK, local_heads, HD
    )
    extended_counts = jnp.concatenate([rim_counts, counts], axis=0)
    extended_valid = position[None, :] < extended_counts[:, None]
    window_keys = jnp.stack(
        [extended_keys[place : place + groups_here] for place in range(PREV + 1)], axis=1
    ).reshape(groups_here, (PREV + 1) * BLK, local_heads, HD)
    window_values = jnp.stack(
        [extended_values[place : place + groups_here] for place in range(PREV + 1)], axis=1
    ).reshape(groups_here, (PREV + 1) * BLK, local_heads, HD)
    window_valid = jnp.stack(
        [extended_valid[place : place + groups_here] for place in range(PREV + 1)], axis=1
    )
    group_on = jnp.concatenate(
        [window_mask[:, ::-1] == 1, jnp.ones((groups_here, 1), jnp.bool_)], axis=1
    )
    causal = position[:, None] >= position[None, :]
    causal_full = jnp.concatenate([jnp.ones((BLK, PREV * BLK), jnp.bool_), causal], axis=1)
    allowed = (window_valid & group_on[:, :, None]).reshape(
        groups_here, 1, (PREV + 1) * BLK
    ) & causal_full[None]
    score_scale = 1.0 / HD**0.5
    scores = (
        jnp.einsum("cthd,cshd->chts", query_blocks, window_keys, preferred_element_type=jnp.float32)
        * score_scale
    )
    scores = jnp.where(allowed[:, None], scores, -1e30)
    largest = jnp.max(scores, axis=-1, keepdims=True)
    expd = jnp.exp(scores - largest)
    weights = (expd / jnp.sum(expd, axis=-1, keepdims=True)).astype(jnp.bfloat16)
    local_part = jnp.einsum(
        "chts,cshd->cthd", weights, window_values, preferred_element_type=jnp.float32
    )
    inter = jnp.einsum(
        "cthd,chde->cthe", query_blocks, prior_rounded, preferred_element_type=jnp.float32
    )
    intra_weights = jnp.einsum(
        "cthd,cshd->chts", query_blocks, key_blocks, preferred_element_type=jnp.float32
    )
    intra_weights = jnp.where(causal[None, None], intra_weights, 0.0).astype(jnp.bfloat16)
    intra = jnp.einsum(
        "chts,cshe->cthe", intra_weights, value_blocks, preferred_element_type=jnp.float32
    )
    linear_part = inter + intra
    local_squares = jnp.sum(linear_part * linear_part, axis=(2, 3))
    row_squares = lax.psum(local_squares, "outer")
    normed = linear_part * lax.rsqrt(row_squares / WIDTH + 1e-06)[:, :, None, None]
    result = normed * norm_gain.reshape(local_heads, HD)[None, None] + local_part
    return result.reshape(tok_rows, local_heads * HD).astype(jnp.bfloat16)


def solution(mesh):
    return jax.shard_map(
        shards,
        mesh=mesh,
        in_specs=(
            P("inner", "outer"),
            P("inner", "outer"),
            P("inner", "outer"),
            P("inner"),
            P("inner", None),
            P("outer"),
        ),
        out_specs=P("inner", "outer"),
        check_vma=False,
    )
```

profile of v0, /device:TPU:7, one launch (start us, length us, event | category | flops | bytes accessed | tf_op | source)
XLA Modules:
  0.0 166.0 jit_solution(16054141134522092386)
XLA Ops:
  6.5 0.7 fusion.27
  7.3 1.2 broadcast_select_fusion
  8.7 1.2 reshape.85
  10.8 1.1 fusion.38
  12.0 0.7 slice.70
  12.7 0.7 slice.79
  13.4 4.0 %collective-permute-start.2 = (bf16[384,256]{1,0:T(8,128)(2,1)}, bf16[384,256]{1,0:T(8,128)(2,1)S(1)}, u32[]{:S(2)}, u32[]{:S(2)}) collective-permute-start(bf16[384,256]{1,0:T(8,128)(2,1)} %slice.79), channel_id=1, source_target_pairs={{0,1},{1,2},{2,3},{3,4},{4,5},{5,6},{6,7},{7,8},{8,9},{9,10},{10,1... | collective-permute-start | bytes 589832 | tf_op jit(solution)/shard_map/ppermute | solution.py:26
  18.1 4.0 %collective-permute-start.1 = (s32[3]{0:T(128)}, s32[3]{0:T(128)}, u32[]{:S(2)}, u32[]{:S(2)}) collective-permute-start(s32[3]{0:T(128)} %slice.61), channel_id=1, source_target_pairs={{0,1},{1,2},{2,3},{3,4},{4,5},{5,6},{6,7},{7,8},{8,9},{9,10},{10,1... | collective-permute-start | bytes 44 | tf_op jit(solution)/shard_map/ppermute | solution.py:26
  22.1 0.7 slice.57
  22.8 4.0 %collective-permute-start = (bf16[384,256]{1,0:T(8,128)(2,1)}, bf16[384,256]{1,0:T(8,128)(2,1)S(1)}, u32[]{:S(2)}, u32[]{:S(2)}) collective-permute-start(bf16[384,256]{1,0:T(8,128)(2,1)} %slice.57), channel_id=1, source_target_pairs={{0,1},{1,2},{2,3},{3,4},{4,5},{5,6},{6,7},{7,8},{8,9},{9,10},{10,1... | collective-permute-start | bytes 589832 | tf_op jit(solution)/shard_map/ppermute | solution.py:26
  26.8 0.9 stack.58
  27.7 0.9 stack.48
  28.6 2.0 %copy.56 = bf16[8,1,128,2,128]{4,2,1,3,0:T(8,128)(2,1)} copy(bf16[8,1,128,2,128]{4,3,2,0,1:T(2,128)(2,1)} %stack.58) | data formatting | bytes 1048576 | tf_op jit(solution)/shard_map/stack | solution.py:69
  30.6 1.2 reshape.86
  31.9 3.8 %copy.52 = bf16[8,1,128,2,128]{2,1,4,3,0:T(2,128)(2,1)} copy(bf16[8,1,128,2,128]{4,3,2,0,1:T(2,128)(2,1)} %stack.48) | data formatting | bytes 1048576 | tf_op jit(solution)/shard_map/stack | solution.py:72
  35.7 0.7 pad_add_fusion
  36.6 1.4 broadcast_and_fusion
  38.0 0.9 fusion.13
  38.9 1.2 stack.55
  40.0 0.9 copy.53
  41.1 0.9 copy.54
  42.1 0.9 copy.55
  43.1 1.1 fusion.32
  44.2 1.2 stack.45
  45.4 2.0 %copy.49 = bf16[8,1,128,2,128]{2,1,4,3,0:T(2,128)(2,1)} copy(bf16[8,1,128,2,128]{4,3,2,0,1:T(2,128)(2,1)S(1)} %stack.45) | data formatting | bytes 1048576 | tf_op jit(solution)/shard_map/stack | solution.py:72
  47.4 1.2 stack.46
  48.6 2.0 %copy.50 = bf16[8,1,128,2,128]{2,1,4,3,0:T(2,128)(2,1)} copy(bf16[8,1,128,2,128]{4,3,2,0,1:T(2,128)(2,1)S(1)} %stack.46) | data formatting | bytes 1048576 | tf_op jit(solution)/shard_map/stack | solution.py:72
  50.7 2.0 %copy.51 = bf16[8,1,128,2,128]{2,1,4,3,0:T(2,128)(2,1)} copy(bf16[8,1,128,2,128]{4,3,2,0,1:T(2,128)(2,1)S(1)} %stack.47) | data formatting | bytes 1048576 | tf_op jit(solution)/shard_map/stack | solution.py:72
  52.7 6.4 %pad_maximum_fusion = bf16[8,4,128,2,128]{2,1,4,3,0:T(4,128)(2,1)S(1)} fusion(bf16[8,1,128,2,128]{2,1,4,3,0:T(2,128)(2,1)} %copy.52, bf16[8,1,128,2,128]{2,1,4,3,0:T(2,128)(2,1)} %copy.51, bf16[8,1,128,2,128]{2,1,4,3,0:T(2,128)(2,1)} %copy.50, bf16[8,1,128,2,128]{2,1,4,3,0:T(2,128)(2,1)} %copy.49), kind=kLoop, calls=%fused_computation.6 | loop fusion | flops 8388608 | bytes 4194304 | tf_op jit(solution)/shard_map/stack | solution.py:72
  59.1 2.2 %reshape.87 = bf16[8,512,2,128]{1,3,2,0:T(8,128)(2,1)} reshape(bf16[8,4,128,2,128]{2,1,4,3,0:T(4,128)(2,1)S(1)} %pad_maximum_fusion) | data formatting | bytes 4194304 | tf_op jit(solution)/shard_map/reshape | solution.py:74
  61.3 1.8 %pad_maximum_fusion.1 = bf16[8,4,128,2,128]{4,2,1,3,0:T(8,128)(2,1)S(1)} fusion(bf16[8,1,128,2,128]{4,2,1,3,0:T(8,128)(2,1)} %copy.56, bf16[8,1,128,2,128]{4,2,1,3,0:T(8,128)(2,1)} %copy.55, bf16[8,1,128,2,128]{4,2,1,3,0:T(8,128)(2,1)} %copy.54, bf16[8,1,128,2,128]{4,2,1,3,0:T(8,128)(2,1)} %copy.53), kind=kLoop, calls=%fused_computation.7 | loop fusion | flops 3145728 | bytes 4194304 | tf_op jit(solution)/shard_map/stack | solution.py:69
  63.1 0.7 fusion.21
  64.2 3.9 %fusion.33 = (f32[8,2,128]{2,1,0:T(2,128)S(1)}, f32[8,2,128,512]{2,3,1,0:T(8,128)}) fusion(f32[8,2,512,128]{3,2,1,0:T(8,128)S(1)} %fusion.21, pred[8,128,512]{1,2,0:T(8,128)(4,1)S(1)} %copy-done.4), kind=kOutput, calls=%fused_computation.63 | output fusion | flops 6291967 | bytes 8921088 | tf_op jit(solution)/shard_map/sub | solution.py:93
  68.0 32.9 %all-gather.2.cloned.1.call-done = f32[32,2,128,128]{3,2,1,0:T(8,128)} async-done(((f32[1,2,128,128]{3,2,1,0:T(8,128)}), f32[32,2,128,128]{3,2,1,0:T(8,128)}) %all-gather.2.cloned.1.call-update) | async-done | bytes 4194320 | tf_op jit(solution)/shard_map/all_gather | solution.py:14
  100.9 23.1 %while.10 = (s32[]{:T(128)}, f32[2,128,128]{2,1,0:T(8,128)S(1)}, s32[]{:T(128)}, f32[32,2,128,128]{3,2,1,0:T(8,128)}, s32[]{:T(128)}, /*index=5*/s32[]{:T(128)}, s32[]{:T(128)}) while((s32[]{:T(128)}, f32[2,128,128]{2,1,0:T(8,128)S(1)}, s32[]{:T(128)}, f32[32,2,128,128]{3,2,1,0:T(8,128)}, s32[]{:T(128)}, /*index=5*/s32[]{:T(128)}, ...), condition=%wide.region_2.3_spmd, body=%wide.region_1.2_spmd.sunk | while | flops 32773 | bytes 393331 | solution.py:20
  101.0 0.9 bitcast_add_fusion.2
  101.9 0.9 bitcast_add_fusion.2
  102.9 0.9 bitcast_add_fusion.2
  103.9 0.9 bitcast_add_fusion.2
  104.8 0.9 bitcast_add_fusion.2
  105.8 0.9 bitcast_add_fusion.2
  106.8 0.9 bitcast_add_fusion.2
  107.7 0.9 bitcast_add_fusion.2
  108.7 0.9 bitcast_add_fusion.2
  109.7 0.9 bitcast_add_fusion.2
  110.6 0.9 bitcast_add_fusion.2
  111.6 0.9 bitcast_add_fusion.2
  112.5 0.9 bitcast_add_fusion.2
  113.5 0.9 bitcast_add_fusion.2
  114.5 0.9 bitcast_add_fusion.2
  115.4 0.9 bitcast_add_fusion.2
  116.4 0.9 bitcast_add_fusion.2
  117.4 0.9 bitcast_add_fusion.2
  118.3 0.9 bitcast_add_fusion.2
  119.3 0.9 bitcast_add_fusion.2
  120.3 0.9 bitcast_add_fusion.2
  121.2 0.9 bitcast_add_fusion.2
  122.2 0.9 bitcast_add_fusion.2
  123.2 0.9 bitcast_add_fusion.2
  124.1 1.5 convolution_bitcast_fusion.2
  125.6 1.9 %multiply_reduce_fusion = (f32[8,128]{1,0:T(8,128)S(1)}, f32[8,128,2,128]{1,3,2,0:T(8,128)S(1)}) fusion(f32[8,128,2,128]{1,3,2,0:T(8,128)} %convolution_bitcast_fusion.2, bf16[8,128,2,128]{1,3,2,0:T(8,128)(2,1)S(1)} %copy-done.2, pred[128,128]{0,1:T(8,128)(4,1)S(1)} %iota_compare_fusion, bf16[8,128,2,128]{3,2,1,0:T(2,128)(2,1)S(1)} %reshape.84, ...), kind=kOutput, calls=%fused_computation.21 | convolution fusion | flops 135527424 | bytes 3690496 | tf_op jit(solution)/shard_map/chts,cshe->cthe/dot_general | solution.py:105
  127.5 26.7 %psum.7 = f32[8,128]{1,0:T(8,128)S(1)} all-reduce(f32[8,128]{1,0:T(8,128)S(1)} %get-tuple-element.49), channel_id=1, replica_groups=mesh['outer'=16,'inner'=32] {'outer'}, use_global_device_ids=true, to_apply=%region_4.5 | all-reduce | flops 1024 | bytes 8192 | tf_op jit(solution)/shard_map/psum | solution.py:110
  154.2 3.5 %fusion.10 = bf16[8,128,2,128]{1,3,2,0:T(8,128)(2,1)S(1)} fusion(bf16[8,512,2,128]{1,3,2,0:T(8,128)(2,1)} %reshape.87, f32[8,2,128,512]{2,3,1,0:T(8,128)} %get-tuple-element.48, f32[8,2,128]{2,1,0:T(2,128)S(1)} %get-tuple-element.47, f32[8,128,2,128]{1,3,2,0:T(8,128)S(1)} %get-tuple-element.50, f32[2,128]{1,0:T(2,128)S(1)} %bitcast.65, ...), kind=kOutput, calls=%fused_computation.19 | convolution fusion | flops 271581184 | bytes 7877632 | tf_op jit(solution)/shard_map/chts,cshd->cthd/dot_general | solution.py:95
  158.2 0.9 copy.84
  (43 shorter events, 3.2 us)
Async XLA Ops:
  6.5 94.4 %all-gather.2.cloned.1.call-start = ((), (), s32[]{:S(2)}) async-start(), calls=%async_computation | async-start | bytes 4325376 | tf_op jit(solution)/shard_map/all_gather | solution.py:14
  8.5 8.9 %copy-start.7 = (s32[8]{0:T(128)S(1)}, s32[8]{0:T(128)}, u32[]{:S(2)}) copy-start(s32[8]{0:T(128)} %param.11) | copy-start | bytes 100
  8.5 13.5 %copy-start = (bf16[1024,256]{1,0:T(8,128)(2,1)S(1)}, bf16[1024,256]{1,0:T(8,128)(2,1)}, u32[]{:S(2)}) copy-start(bf16[1024,256]{1,0:T(8,128)(2,1)} %param.10) | copy-start | bytes 1572868
  10.3 18.3 %copy-start.1 = (bf16[8,128,2,128]{1,3,2,0:T(8,128)(2,1)}, bf16[8,128,2,128]{1,3,2,0:T(8,128)(2,1)S(1)}, u32[]{:S(2)}) copy-start(bf16[8,128,2,128]{1,3,2,0:T(8,128)(2,1)S(1)} %copy.48) | copy-start | bytes 1572868
  10.8 20.9 %copy-start.5 = (s32[8,3]{0,1:T(4,128)S(1)}, s32[8,3]{0,1:T(4,128)}, u32[]{:S(2)}) copy-start(s32[8,3]{0,1:T(4,128)} %param.12) | copy-start | bytes 292
  11.9 16.6 %copy-start.3 = (f32[8,2,128,128]{3,2,1,0:T(8,128)}, f32[8,2,128,128]{3,2,1,0:T(8,128)S(1)}, u32[]{:S(2)}) copy-start(f32[8,2,128,128]{3,2,1,0:T(8,128)S(1)} %fusion.38) | copy-start | bytes 3145732
  13.4 24.6 %collective-permute-start.2 = (bf16[384,256]{1,0:T(8,128)(2,1)}, bf16[384,256]{1,0:T(8,128)(2,1)S(1)}, u32[]{:S(2)}, u32[]{:S(2)}) collective-permute-start(bf16[384,256]{1,0:T(8,128)(2,1)} %slice.79), channel_id=1, source_target_pairs={{0,1},{1,2},{2,3},{3,4},{4,5},{5,6},{6,7},{7,8},{8,9},{9,10},{10,1... | collective-permute-start | bytes 589832 | tf_op jit(solution)/shard_map/ppermute | solution.py:26
  18.1 17.6 %collective-permute-start.1 = (s32[3]{0:T(128)}, s32[3]{0:T(128)}, u32[]{:S(2)}, u32[]{:S(2)}) collective-permute-start(s32[3]{0:T(128)} %slice.61), channel_id=1, source_target_pairs={{0,1},{1,2},{2,3},{3,4},{4,5},{5,6},{6,7},{7,8},{8,9},{9,10},{10,1... | collective-permute-start | bytes 44 | tf_op jit(solution)/shard_map/ppermute | solution.py:26
  22.8 20.3 %collective-permute-start = (bf16[384,256]{1,0:T(8,128)(2,1)}, bf16[384,256]{1,0:T(8,128)(2,1)S(1)}, u32[]{:S(2)}, u32[]{:S(2)}) collective-permute-start(bf16[384,256]{1,0:T(8,128)(2,1)} %slice.57), channel_id=1, source_target_pairs={{0,1},{1,2},{2,3},{3,4},{4,5},{5,6},{6,7},{7,8},{8,9},{9,10},{10,1... | collective-permute-start | bytes 589832 | tf_op jit(solution)/shard_map/ppermute | solution.py:26
  63.1 1.0 copy-start.4
  64.2 59.9 %slice-start = ((f32[8,2,128,128]{3,2,1,0:T(8,128)}), f32[7,2,128,128]{3,2,1,0:T(8,128)S(1)}, s32[]{:S(2)}) async-start(f32[8,2,128,128]{3,2,1,0:T(8,128)} %copy-done.3), calls=%async_computation.1 | async-start | bytes 1835008 | tf_op jit(solution)/shard_map/slice | solution.py:47
  68.0 57.6 %copy-start.2 = (bf16[8,128,2,128]{1,3,2,0:T(8,128)(2,1)S(1)}, bf16[8,128,2,128]{1,3,2,0:T(8,128)(2,1)}, u32[]{:S(2)}) copy-start(bf16[8,128,2,128]{1,3,2,0:T(8,128)(2,1)} %copy-done.1) | copy-start | bytes 1572868
  100.9 53.3 %copy-start.6 = (f32[256]{0:T(256)S(1)}, f32[256]{0:T(256)}, u32[]{:S(2)}) copy-start(f32[256]{0:T(256)} %param.13) | copy-start | bytes 3076
Sparse Core Ops, SparseCore 0:
  12.8 88.0 all-gather.1
where the time goes:
time: 167 us; the launch traced here: 166 us
  other arithmetic  40.8 us (24%)
  waiting for transfers between devices  32.9 us (20%)
  local copies, waits for them, and re-layouts  31 us (19%)
  blocking collectives  26.7 us (16%)
  between operations  13.6 us (8%)
  starting transfers between devices  12 us (7%)
  matrix products  8.16 us (5%)
    all_gather x1, waiting for transfers between devices, carried_in(): gathered = lax.all_gather(part, axis)  32.9 us
    psum x1, blocking collectives, shards(): row_squares = lax.psum(local_squares, 'outer')  26.7 us
    add x24, other arithmetic, add_states(): return earlier + later  22.5 us
    another operation x8, local copies, waits for them, and re-layouts, shards(): jnp.stack([extended_values[place:place + groups_here] for place in range(...  13.2 us
    ppermute x3, starting transfers between devices, from_behind(): lax.ppermute(value, axis, [(source, source + steps) for source in range(f...  12 us
    another operation x8, local copies, waits for them, and re-layouts, shards(): jnp.stack([extended_keys[place:place + groups_here] for place in range(PR...  7.08 us
    another operation x1, other arithmetic, shards(): jnp.stack([extended_values[place:place + groups_here] for place in range(...  6.43 us
    sub x1, other arithmetic, shards(): expd = jnp.exp(scores - largest)  3.88 us
  transfers between devices with their start and end apart: 4, of which 1 were waited for; matrix products, arithmetic and copies ran while one was open for 26% of the time, Pallas kernels for 0%

commit v1 on v0

--- a/solution.py
+++ b/solution.py
@@ -107,7 +107,7 @@
     )
     linear_part = inter + intra
     local_squares = jnp.sum(linear_part * linear_part, axis=(2, 3))
-    row_squares = lax.psum(local_squares, "outer")
+    row_squares = jnp.sum(lax.all_gather(local_squares, "outer"), 0)
     normed = linear_part * lax.rsqrt(row_squares / WIDTH + 1e-06)[:, :, None, None]
     result = normed * norm_gain.reshape(local_heads, HD)[None, None] + local_part
     return result.reshape(tok_rows, local_heads * HD).astype(jnp.bfloat16)

time: 167 us -> 161 us (0.964)
  blocking collectives: 26.7 us -> 20.8 us
    psum x1 -> x0, blocking collectives: 26.7 us -> none  [shards(): row_squares = lax.psum(local_squares, 'outer')]
    all_gather x0 -> x1, blocking collectives: none -> 20.8 us  [shards(): row_squares = jnp.sum(lax.all_gather(local_squares, 'outer'), 0)]
  transfers between devices with their start and end apart: 4 -> 4, of which waited for: 1 -> 1; matrix products, arithmetic and copies ran while one was open for 26% -> 27% of each run, Pallas kernels for 0% -> 0%
where the time goes in v1:
time: 161 us; the launch traced here: 160 us
  other arithmetic  40.9 us (25%)
  waiting for transfers between devices  32.9 us (20%)
  local copies, waits for them, and re-layouts  31 us (19%)
  blocking collectives  20.8 us (13%)
  between operations  13.7 us (9%)
  starting transfers between devices  12 us (7%)
  matrix products  8.16 us (5%)
    all_gather x1, waiting for transfers between devices, carried_in(): gathered = lax.all_gather(part, axis)  32.9 us
    add x24, other arithmetic, add_states(): return earlier + later  22.5 us
    all_gather x1, blocking collectives, shards(): row_squares = jnp.sum(lax.all_gather(local_squares, 'outer'), 0)  20.8 us
    another operation x8, local copies, waits for them, and re-layouts, shards(): jnp.stack([extended_values[place:place + groups_here] for place in range(...  13.2 us
    ppermute x3, starting transfers between devices, from_behind(): lax.ppermute(value, axis, [(source, source + steps) for source in range(f...  12 us
    another operation x8, local copies, waits for them, and re-layouts, shards(): jnp.stack([extended_keys[place:place + groups_here] for place in range(PR...  7.08 us
    another operation x1, other arithmetic, shards(): jnp.stack([extended_values[place:place + groups_here] for place in range(...  6.43 us
    sub x1, other arithmetic, shards(): expd = jnp.exp(scores - largest)  3.88 us
  transfers between devices with their start and end apart: 4, of which 1 were waited for; matrix products, arithmetic and copies ran while one was open for 27% of the time, Pallas kernels for 0%

profile of v1, /device:TPU:7, one launch (start us, length us, event | category | flops | bytes accessed | tf_op | source)
XLA Modules:
  0.0 160.0 jit_solution(15511953102851819945)
XLA Ops:
  6.5 0.7 fusion.27
  7.3 1.2 broadcast_select_fusion
  8.7 1.2 reshape.89
  10.8 1.1 fusion.38
  12.0 0.7 slice.70
  12.7 0.7 slice.79
  13.4 4.0 %collective-permute-start.2 = (bf16[384,256]{1,0:T(8,128)(2,1)}, bf16[384,256]{1,0:T(8,128)(2,1)S(1)}, u32[]{:S(2)}, u32[]{:S(2)}) collective-permute-start(bf16[384,256]{1,0:T(8,128)(2,1)} %slice.79), channel_id=1, source_target_pairs={{0,1},{1,2},{2,3},{3,4},{4,5},{5,6},{6,7},{7,8},{8,9},{9,10},{10,1... | collective-permute-start | bytes 589832 | tf_op jit(solution)/shard_map/ppermute | solution.py:26
  18.1 4.0 %collective-permute-start.1 = (s32[3]{0:T(128)}, s32[3]{0:T(128)}, u32[]{:S(2)}, u32[]{:S(2)}) collective-permute-start(s32[3]{0:T(128)} %slice.61), channel_id=1, source_target_pairs={{0,1},{1,2},{2,3},{3,4},{4,5},{5,6},{6,7},{7,8},{8,9},{9,10},{10,1... | collective-permute-start | bytes 44 | tf_op jit(solution)/shard_map/ppermute | solution.py:26
  22.1 0.7 slice.57
  22.8 4.0 %collective-permute-start = (bf16[384,256]{1,0:T(8,128)(2,1)}, bf16[384,256]{1,0:T(8,128)(2,1)S(1)}, u32[]{:S(2)}, u32[]{:S(2)}) collective-permute-start(bf16[384,256]{1,0:T(8,128)(2,1)} %slice.57), channel_id=1, source_target_pairs={{0,1},{1,2},{2,3},{3,4},{4,5},{5,6},{6,7},{7,8},{8,9},{9,10},{10,1... | collective-permute-start | bytes 589832 | tf_op jit(solution)/shard_map/ppermute | solution.py:26
  26.8 0.9 stack.58
  27.7 0.9 stack.48
  28.6 2.0 %copy.76 = bf16[8,1,128,2,128]{4,2,1,3,0:T(8,128)(2,1)} copy(bf16[8,1,128,2,128]{4,3,2,0,1:T(2,128)(2,1)} %stack.58) | data formatting | bytes 1048576 | tf_op jit(solution)/shard_map/stack | solution.py:69
  30.6 1.2 reshape.90
  31.9 3.8 %copy.72 = bf16[8,1,128,2,128]{2,1,4,3,0:T(2,128)(2,1)} copy(bf16[8,1,128,2,128]{4,3,2,0,1:T(2,128)(2,1)} %stack.48) | data formatting | bytes 1048576 | tf_op jit(solution)/shard_map/stack | solution.py:72
  35.7 0.7 pad_add_fusion
  36.6 1.4 broadcast_and_fusion
  38.0 0.9 fusion.13
  38.9 1.2 stack.55
  40.0 0.9 copy.73
  41.1 0.9 copy.74
  42.1 0.9 copy.75
  43.1 1.1 fusion.32
  44.2 1.2 stack.45
  45.4 2.0 %copy.69 = bf16[8,1,128,2,128]{2,1,4,3,0:T(2,128)(2,1)} copy(bf16[8,1,128,2,128]{4,3,2,0,1:T(2,128)(2,1)S(1)} %stack.45) | data formatting | bytes 1048576 | tf_op jit(solution)/shard_map/stack | solution.py:72
  47.4 1.2 stack.46
  48.6 2.0 %copy.70 = bf16[8,1,128,2,128]{2,1,4,3,0:T(2,128)(2,1)} copy(bf16[8,1,128,2,128]{4,3,2,0,1:T(2,128)(2,1)S(1)} %stack.46) | data formatting | bytes 1048576 | tf_op jit(solution)/shard_map/stack | solution.py:72
  50.7 2.0 %copy.71 = bf16[8,1,128,2,128]{2,1,4,3,0:T(2,128)(2,1)} copy(bf16[8,1,128,2,128]{4,3,2,0,1:T(2,128)(2,1)S(1)} %stack.47) | data formatting | bytes 1048576 | tf_op jit(solution)/shard_map/stack | solution.py:72
  52.7 6.4 %pad_maximum_fusion = bf16[8,4,128,2,128]{2,1,4,3,0:T(4,128)(2,1)S(1)} fusion(bf16[8,1,128,2,128]{2,1,4,3,0:T(2,128)(2,1)} %copy.72, bf16[8,1,128,2,128]{2,1,4,3,0:T(2,128)(2,1)} %copy.71, bf16[8,1,128,2,128]{2,1,4,3,0:T(2,128)(2,1)} %copy.70, bf16[8,1,128,2,128]{2,1,4,3,0:T(2,128)(2,1)} %copy.69), kind=kLoop, calls=%fused_computation.6 | loop fusion | flops 8388608 | bytes 4194304 | tf_op jit(solution)/shard_map/stack | solution.py:72
  59.1 2.2 %reshape.91 = bf16[8,512,2,128]{1,3,2,0:T(8,128)(2,1)} reshape(bf16[8,4,128,2,128]{2,1,4,3,0:T(4,128)(2,1)S(1)} %pad_maximum_fusion) | data formatting | bytes 4194304 | tf_op jit(solution)/shard_map/reshape | solution.py:74
  61.3 1.8 %pad_maximum_fusion.1 = bf16[8,4,128,2,128]{4,2,1,3,0:T(8,128)(2,1)S(1)} fusion(bf16[8,1,128,2,128]{4,2,1,3,0:T(8,128)(2,1)} %copy.76, bf16[8,1,128,2,128]{4,2,1,3,0:T(8,128)(2,1)} %copy.75, bf16[8,1,128,2,128]{4,2,1,3,0:T(8,128)(2,1)} %copy.74, bf16[8,1,128,2,128]{4,2,1,3,0:T(8,128)(2,1)} %copy.73), kind=kLoop, calls=%fused_computation.7 | loop fusion | flops 3145728 | bytes 4194304 | tf_op jit(solution)/shard_map/stack | solution.py:69
  63.1 0.7 fusion.21
  64.2 3.9 %fusion.33 = (f32[8,2,128]{2,1,0:T(2,128)S(1)}, f32[8,2,128,512]{2,3,1,0:T(8,128)}) fusion(f32[8,2,512,128]{3,2,1,0:T(8,128)S(1)} %fusion.21, pred[8,128,512]{1,2,0:T(8,128)(4,1)S(1)} %copy-done.4), kind=kOutput, calls=%fused_computation.64 | output fusion | flops 6291967 | bytes 8921088 | tf_op jit(solution)/shard_map/sub | solution.py:93
  68.0 32.9 %all-gather.3.cloned.1.call-done = f32[32,2,128,128]{3,2,1,0:T(8,128)} async-done(((f32[1,2,128,128]{3,2,1,0:T(8,128)}), f32[32,2,128,128]{3,2,1,0:T(8,128)}) %all-gather.3.cloned.1.call-update) | async-done | bytes 4194320 | tf_op jit(solution)/shard_map/all_gather | solution.py:14
  100.9 23.1 %while.10 = (s32[]{:T(128)}, f32[2,128,128]{2,1,0:T(8,128)S(1)}, s32[]{:T(128)}, f32[32,2,128,128]{3,2,1,0:T(8,128)}, s32[]{:T(128)}, /*index=5*/s32[]{:T(128)}, s32[]{:T(128)}) while((s32[]{:T(128)}, f32[2,128,128]{2,1,0:T(8,128)S(1)}, s32[]{:T(128)}, f32[32,2,128,128]{3,2,1,0:T(8,128)}, s32[]{:T(128)}, /*index=5*/s32[]{:T(128)}, ...), condition=%wide.region_2.3_spmd, body=%wide.region_1.2_spmd.sunk | while | flops 32773 | bytes 393331 | solution.py:20
  101.0 0.9 bitcast_add_fusion.2
  101.9 0.9 bitcast_add_fusion.2
  102.9 0.9 bitcast_add_fusion.2
  103.9 0.9 bitcast_add_fusion.2
  104.8 0.9 bitcast_add_fusion.2
  105.8 0.9 bitcast_add_fusion.2
  106.8 0.9 bitcast_add_fusion.2
  107.7 0.9 bitcast_add_fusion.2
  108.7 0.9 bitcast_add_fusion.2
  109.7 0.9 bitcast_add_fusion.2
  110.6 0.9 bitcast_add_fusion.2
  111.6 0.9 bitcast_add_fusion.2
  112.5 0.9 bitcast_add_fusion.2
  113.5 0.9 bitcast_add_fusion.2
  114.5 0.9 bitcast_add_fusion.2
  115.4 0.9 bitcast_add_fusion.2
  116.4 0.9 bitcast_add_fusion.2
  117.4 0.9 bitcast_add_fusion.2
  118.3 0.9 bitcast_add_fusion.2
  119.3 0.9 bitcast_add_fusion.2
  120.3 0.9 bitcast_add_fusion.2
  121.2 0.9 bitcast_add_fusion.2
  122.2 0.9 bitcast_add_fusion.2
  123.2 0.9 bitcast_add_fusion.2
  124.1 1.5 convolution_bitcast_fusion.2
  125.6 1.9 %multiply_reduce_fusion = (f32[8,128]{1,0:T(8,128)S(1)}, f32[8,128,2,128]{1,3,2,0:T(8,128)S(1)}) fusion(f32[8,128,2,128]{1,3,2,0:T(8,128)} %convolution_bitcast_fusion.2, bf16[8,128,2,128]{1,3,2,0:T(8,128)(2,1)S(1)} %copy-done.2, pred[128,128]{0,1:T(8,128)(4,1)S(1)} %iota_compare_fusion, bf16[8,128,2,128]{3,2,1,0:T(2,128)(2,1)S(1)} %reshape.88, ...), kind=kOutput, calls=%fused_computation.21 | convolution fusion | flops 135527424 | bytes 3690496 | tf_op jit(solution)/shard_map/chts,cshe->cthe/dot_general | solution.py:105
  127.5 20.8 %all-gather = f32[128,128]{1,0:T(8,128)S(1)} all-gather(f32[8,128]{1,0:T(8,128)S(1)} %get-tuple-element.49), channel_id=2, replica_groups=mesh['outer'=16,'inner'=32] {'outer'}, dimensions={0}, use_global_device_ids=true | all-gather | bytes 69632 | tf_op jit(solution)/shard_map/all_gather | solution.py:110
  148.3 3.5 %fusion.10 = bf16[8,128,2,128]{1,3,2,0:T(8,128)(2,1)S(1)} fusion(bf16[8,512,2,128]{1,3,2,0:T(8,128)(2,1)} %reshape.91, f32[8,2,128,512]{2,3,1,0:T(8,128)} %get-tuple-element.48, f32[8,2,128]{2,1,0:T(2,128)S(1)} %get-tuple-element.47, f32[8,128,2,128]{1,3,2,0:T(8,128)S(1)} %get-tuple-element.50, f32[2,128]{1,0:T(2,128)S(1)} %bitcast.67, ...), kind=kOutput, calls=%fused_computation.19 | convolution fusion | flops 271581184 | bytes 7877632 | tf_op jit(solution)/shard_map/chts,cshd->cthd/dot_general | solution.py:95
  152.3 0.9 copy.104
  (44 shorter events, 3.2 us)
Async XLA Ops:
  6.5 94.4 %all-gather.3.cloned.1.call-start = ((), (), s32[]{:S(2)}) async-start(), calls=%async_computation | async-start | bytes 4325376 | tf_op jit(solution)/shard_map/all_gather | solution.py:14
  8.5 8.9 %copy-start.7 = (s32[8]{0:T(128)S(1)}, s32[8]{0:T(128)}, u32[]{:S(2)}) copy-start(s32[8]{0:T(128)} %param.11) | copy-start | bytes 100
  8.5 13.5 %copy-start = (bf16[1024,256]{1,0:T(8,128)(2,1)S(1)}, bf16[1024,256]{1,0:T(8,128)(2,1)}, u32[]{:S(2)}) copy-start(bf16[1024,256]{1,0:T(8,128)(2,1)} %param.10) | copy-start | bytes 1572868
  10.3 18.3 %copy-start.1 = (bf16[8,128,2,128]{1,3,2,0:T(8,128)(2,1)}, bf16[8,128,2,128]{1,3,2,0:T(8,128)(2,1)S(1)}, u32[]{:S(2)}) copy-start(bf16[8,128,2,128]{1,3,2,0:T(8,128)(2,1)S(1)} %copy.68) | copy-start | bytes 1572868
  10.8 20.9 %copy-start.5 = (s32[8,3]{0,1:T(4,128)S(1)}, s32[8,3]{0,1:T(4,128)}, u32[]{:S(2)}) copy-start(s32[8,3]{0,1:T(4,128)} %param.12) | copy-start | bytes 292
  11.9 16.6 %copy-start.3 = (f32[8,2,128,128]{3,2,1,0:T(8,128)}, f32[8,2,128,128]{3,2,1,0:T(8,128)S(1)}, u32[]{:S(2)}) copy-start(f32[8,2,128,128]{3,2,1,0:T(8,128)S(1)} %fusion.38) | copy-start | bytes 3145732
  13.4 24.6 %collective-permute-start.2 = (bf16[384,256]{1,0:T(8,128)(2,1)}, bf16[384,256]{1,0:T(8,128)(2,1)S(1)}, u32[]{:S(2)}, u32[]{:S(2)}) collective-permute-start(bf16[384,256]{1,0:T(8,128)(2,1)} %slice.79), channel_id=1, source_target_pairs={{0,1},{1,2},{2,3},{3,4},{4,5},{5,6},{6,7},{7,8},{8,9},{9,10},{10,1... | collective-permute-start | bytes 589832 | tf_op jit(solution)/shard_map/ppermute | solution.py:26
  18.1 17.6 %collective-permute-start.1 = (s32[3]{0:T(128)}, s32[3]{0:T(128)}, u32[]{:S(2)}, u32[]{:S(2)}) collective-permute-start(s32[3]{0:T(128)} %slice.61), channel_id=1, source_target_pairs={{0,1},{1,2},{2,3},{3,4},{4,5},{5,6},{6,7},{7,8},{8,9},{9,10},{10,1... | collective-permute-start | bytes 44 | tf_op jit(solution)/shard_map/ppermute | solution.py:26
  22.8 20.3 %collective-permute-start = (bf16[384,256]{1,0:T(8,128)(2,1)}, bf16[384,256]{1,0:T(8,128)(2,1)S(1)}, u32[]{:S(2)}, u32[]{:S(2)}) collective-permute-start(bf16[384,256]{1,0:T(8,128)(2,1)} %slice.57), channel_id=1, source_target_pairs={{0,1},{1,2},{2,3},{3,4},{4,5},{5,6},{6,7},{7,8},{8,9},{9,10},{10,1... | collective-permute-start | bytes 589832 | tf_op jit(solution)/shard_map/ppermute | solution.py:26
  63.1 1.0 copy-start.4
  64.2 59.9 %slice-start = ((f32[8,2,128,128]{3,2,1,0:T(8,128)}), f32[7,2,128,128]{3,2,1,0:T(8,128)S(1)}, s32[]{:S(2)}) async-start(f32[8,2,128,128]{3,2,1,0:T(8,128)} %copy-done.3), calls=%async_computation.1 | async-start | bytes 1835008 | tf_op jit(solution)/shard_map/slice | solution.py:47
  68.0 57.6 %copy-start.2 = (bf16[8,128,2,128]{1,3,2,0:T(8,128)(2,1)S(1)}, bf16[8,128,2,128]{1,3,2,0:T(8,128)(2,1)}, u32[]{:S(2)}) copy-start(bf16[8,128,2,128]{1,3,2,0:T(8,128)(2,1)} %copy-done.1) | copy-start | bytes 1572868
  100.9 47.4 %copy-start.6 = (f32[256]{0:T(256)S(1)}, f32[256]{0:T(256)}, u32[]{:S(2)}) copy-start(f32[256]{0:T(256)} %param.13) | copy-start | bytes 3076
Sparse Core Ops, SparseCore 0:
  12.8 88.0 all-gather.2
